TPU v7x, 512 devices: a whole 4x4x16 slice. The times are simulated.
512 devices in a mesh: dp: 32 (over z, y_lo), fsdp: 16 (over x, y_hi, core).
Axes of the slice: x: 4, y: 4 (y_hi: 2, y_lo: 2; y = y_hi * 2 + y_lo), z: 16, core: 2. Of those that a mesh axis runs over, the one named last changes fastest.
Arguments:
- tokens: bfloat16 [65536, 1024], P(('dp', 'fsdp')), may hold values from -6 to 6
- cotangent: bfloat16 [65536, 1024], P(('dp', 'fsdp')), may hold values from -6 to 6
- routes: int32 [65536, 1], P(('dp', 'fsdp')), may hold values from 0 to 32; in each aligned block of 128 rows (0 to 127, 128 to 255, ...) at most 4 rows name the same one
- norm_gain_vector: float32 [1024], replicated, may hold values from 0.25 to 1.75
- up_weight: bfloat16 [1024, 4096], P(None, 'fsdp'), may hold values from -0.1875 to 0.1875
- up_bias: float32 [4096], P('fsdp'), may hold values from -4 to 4
- down_weight: bfloat16 [4096, 1024], P('fsdp'), may hold values from -0.09375 to 0.09375
Outputs:
- input_grad: bfloat16 [65536, 1024], P(('dp', 'fsdp'))
- up_grad: float32 [1024, 4096], P(None, 'fsdp')
- bias_grad: float32 [4096], P('fsdp')
- down_grad: float32 [4096, 1024], P('fsdp')
- gain_grad: float32 [1024], replicated
Inputs may be any that keep to these rules, and one draw needn't show every extreme that they name: `routes`: among the 128 slots of one device no value below 32 appears more than 4 times; the value 32 marks a padding slot.
All inputs are finite; a program needn't handle non-finite values.
Results may differ from a plain program's by a relative error of at most 0.024.
Values may be sent and summed in bfloat16 or wider, within the bound.
A program may use at most 128 MiB of HBM per device.

v0:
```python
import jax
import jax.numpy as jnp
from jax import lax
from jax.sharding import Mesh
from jax.sharding import PartitionSpec as P

DP = ("dp_0", "dp_1")
FSDP = ("fsdp_0", "fsdp_1", "fsdp_2")
ROWS_AXES = ("fsdp_0", "fsdp_1")
DP_FSDP = ("dp_0", "dp_1", "fsdp_0", "fsdp_1", "fsdp_2")


root_two_pi = 0.7978845608
cubic = 0.044715


def side_by_side(arrays, axis, split_dim, concat_dim, along):
    both = jnp.concatenate(arrays, axis=along)
    filled, at, finished = (
        lax.all_to_all(both, axis, split_axis=split_dim, concat_axis=concat_dim, tiled=True),
        0,
        [],
    )
    for a in arrays:
        finished.append(lax.slice_in_dim(filled, at, at + a.shape[along], axis=along))
        at += a.shape[along]
    return tuple(finished)


def gelu_pair(pre):
    inner = root_two_pi * (pre + cubic * pre * pre * pre)
    tangent = jnp.tanh(inner)
    act = 0.5 * pre * (1.0 + tangent)
    slope = 0.5 * (1.0 + tangent) + 0.5 * pre * (1.0 - tangent * tangent) * root_two_pi * (
        1.0 + 3.0 * cubic * pre * pre
    )
    return (act, slope)


def apply_layer_norm(values):
    row_average = jnp.mean(values, axis=1, keepdims=True)
    centered = values - row_average
    variance = jnp.mean(centered * centered, axis=1, keepdims=True)
    inverse_std = 1.0 / jnp.sqrt(variance + 1e-05)
    return (centered * inverse_std, inverse_std)


def shards(tokens, cotangent, routes, norm_gain_vector, up_weight, up_bias, down_weight):
    particle_slot_count = tokens.shape[0]
    dp_size = lax.axis_size(DP)
    capacity = particle_slot_count // dp_size
    up_weight = lax.all_gather(up_weight, "fsdp_2", axis=1, tiled=True)
    down_weight = lax.all_gather(down_weight, "fsdp_2", axis=0, tiled=True)
    up_bias = lax.all_gather(up_bias, "fsdp_2", axis=0, tiled=True)
    target = routes[:, 0]
    matches = (target[:, None] == jnp.arange(dp_size + 1, dtype=jnp.int32)[None, :]).astype(
        jnp.int32
    )
    earlier = jnp.cumsum(matches, axis=0) - matches
    ranked = jnp.sum(earlier * matches, axis=1)
    slot_index = jnp.where(target < dp_size, target * capacity + ranked, -1)
    placing = (
        slot_index[None, :] == jnp.arange(particle_slot_count, dtype=jnp.int32)[:, None]
    ).astype(jnp.bfloat16)
    send_in = jnp.dot(placing, tokens, preferred_element_type=jnp.float32).astype(jnp.bfloat16)
    send_cot = jnp.dot(placing, cotangent, preferred_element_type=jnp.float32).astype(jnp.bfloat16)
    packed_in, packed_cot = side_by_side((send_in, send_cot), DP, 0, 0, 1)
    local_standardized, own_inverse = apply_layer_norm(packed_in.astype(jnp.float32))
    normed_local = (local_standardized * norm_gain_vector).astype(jnp.bfloat16)
    all_cot = lax.all_gather(packed_cot, ROWS_AXES, axis=0, tiled=True)
    gathered_normed_rows = lax.all_gather(normed_local, ROWS_AXES, axis=0, tiled=True)
    pre = jnp.dot(gathered_normed_rows, up_weight, preferred_element_type=jnp.float32) + up_bias
    act_full, slope = gelu_pair(pre)
    act = act_full.astype(jnp.bfloat16)
    act_grad = jnp.einsum("rd,kd->rk", all_cot, down_weight, preferred_element_type=jnp.float32)
    pre_grad = (act_grad * slope).astype(jnp.bfloat16)
    down_part = jnp.einsum("rk,rd->kd", act, all_cot, preferred_element_type=jnp.float32)
    up_part = jnp.einsum(
        "rk,rd->kd", pre_grad, gathered_normed_rows, preferred_element_type=jnp.float32
    )
    bias_part = jnp.sum(pre_grad.astype(jnp.float32), axis=0)
    partial_gain_grad = jnp.sum(up_part * up_weight.T.astype(jnp.float32), axis=0) / norm_gain_vector
    parts = jnp.concatenate([up_part, down_part], axis=1).astype(jnp.bfloat16)
    mine = lax.psum_scatter(parts, "fsdp_2", scatter_dimension=0, tiled=True)
    mine = lax.psum_scatter(mine, DP, scatter_dimension=0, tiled=True)
    whole = lax.all_gather(mine, DP, axis=0, tiled=True).astype(jnp.float32)
    d = up_weight.shape[0]
    up_grad = whole[:, :d].T
    down_grad = whole[:, d:]
    normed_rows_gradient = lax.psum_scatter(
        jnp.einsum("rk,dk->rd", pre_grad, up_weight, preferred_element_type=jnp.float32).astype(
            jnp.bfloat16
        ),
        ROWS_AXES,
        scatter_dimension=0,
        tiled=True,
    ).astype(jnp.float32)
    index = lax.axis_index(FSDP)
    k = bias_part.shape[0] // 2
    wide = jnp.zeros((8, 2 * k), jnp.float32)
    wide = lax.dynamic_update_slice(wide, bias_part[None], (index // 2, 0))
    small = lax.psum(jnp.concatenate([partial_gain_grad, wide.reshape(-1)]), DP_FSDP)
    gain_grad = small[:d]
    bias_grad = lax.dynamic_slice(small[d:], (index * k,), (k,))
    scaled_values = normed_rows_gradient * norm_gain_vector
    final_result = packed_cot.astype(jnp.float32) + own_inverse * (
        scaled_values
        - jnp.mean(scaled_values, axis=1, keepdims=True)
        - local_standardized * jnp.mean(scaled_values * local_standardized, axis=1, keepdims=True)
    )
    return (final_result.astype(jnp.bfloat16), up_grad, bias_grad, down_grad, gain_grad)


def solution(mesh):
    finer = Mesh(
        mesh.devices.reshape(16, 2, 4, 2, 2), ("dp_0", "dp_1", "fsdp_0", "fsdp_1", "fsdp_2")
    )
    return jax.shard_map(
        shards,
        mesh=finer,
        in_specs=(
            P(DP_FSDP, None),
            P(DP_FSDP, None),
            P(DP_FSDP, None),
            P(),
            P(None, FSDP),
            P(FSDP),
            P(FSDP, None),
        ),
        out_specs=(P(DP_FSDP, None), P(None, FSDP), P(FSDP), P(FSDP, None), P()),
        check_vma=False,
    )
```

profile of v0, /device:TPU:2, one launch (start us, length us, event | category | flops | bytes accessed | tf_op | source)
XLA Modules:
  0.0 631.0 jit_solution(15258363506738329338)
XLA Ops:
  7.2 0.8 fusion.26
  8.0 0.2 reduce_window_sum.11
  8.1 0.8 select_reduce_fusion
  9.0 0.7 compare_select_fusion
  9.6 0.2 convolution_convert_fusion.2
  9.9 1.2 convolution_convert_fusion.3
  11.1 1.0 all_to_all.8
  12.1 16.6 %all-to-all-start = ((bf16[32,4,2048]{2,1,0:T(4,128)(2,1)}), bf16[32,4,2048]{2,1,0:T(4,128)(2,1)S(1)}, u32[]{:S(2)}, u32[]{:S(2)}) async-start(bf16[32,4,2048]{2,1,0:T(4,128)(2,1)} %all_to_all.8), calls=%async_computation | async-start | bytes 1048576 | tf_op jit(solution)/shard_map/all_to_all | solution.py:20
  28.7 0.0 all-gather.13.cloned.1.call-start
  28.8 1.0 copy.14
  29.8 0.0 all-gather.13.cloned.1.call-update
  29.8 0.0 all-gather.11.cloned.1.call-start
  29.9 31.9 %all-to-all-done = bf16[32,4,2048]{2,1,0:T(4,128)(2,1)S(1)} async-done(((bf16[32,4,2048]{2,1,0:T(4,128)(2,1)}), bf16[32,4,2048]{2,1,0:T(4,128)(2,1)S(1)}, u32[]{:S(2)}, u32[]{:S(2)}) %all-to-all-start) | async-done | bytes 524320 | tf_op jit(solution)/shard_map/all_to_all | solution.py:20
  61.7 0.1 all_to_all.10
  61.9 0.1 convert_reduce_fusion.1
  62.0 0.2 fusion.24
  62.2 0.9 fusion.18
  63.2 0.0 all-gather.7.cloned.1.call-start
  63.2 0.7 slice.24
  64.0 0.0 all-gather.9.cloned.1.call-start
  64.0 0.5 all-gather.9.cloned.1.call-update
  64.5 0.0 reduce-scatter.6.cloned.1.call-start
  64.6 1.8 all-gather
  66.4 61.5 %all-gather.11.cloned.1.call-done = bf16[1024,1024]{1,0:T(8,128)(2,1)} async-done(((bf16[128,1024]{1,0:T(8,128)(2,1)}), bf16[1024,1024]{1,0:T(8,128)(2,1)}) %all-gather.11.cloned.1.call-update) | async-done | bytes 2097168 | tf_op jit(solution)/shard_map/all_gather | solution.py:71
  127.9 4.4 fusion.33
  132.4 68.8 %all-gather.7.cloned.1.call-done = bf16[1024,1024]{1,0:T(8,128)(2,1)} async-done(((bf16[128,1024]{1,0:T(8,128)(2,1)}), bf16[1024,1024]{1,0:T(8,128)(2,1)}) %all-gather.7.cloned.1.call-update) | async-done | bytes 2097168 | tf_op jit(solution)/shard_map/all_gather | solution.py:70
  201.1 3.6 convolution_convert_fusion.1
  204.8 17.0 %all-gather.9.cloned.1.call-done = bf16[512,1024]{1,0:T(8,128)(2,1)} async-done(((bf16[256,1024]{1,0:T(8,128)(2,1)}), bf16[512,1024]{1,0:T(8,128)(2,1)}) %all-gather.9.cloned.1.call-update) | async-done | bytes 1048592 | tf_op jit(solution)/shard_map/all_gather | solution.py:53
  221.8 5.1 convert_reduce_fusion
  226.9 1.3 fusion.7
  228.2 1.5 pad_maximum_fusion
  229.7 0.0 reduce-scatter.8.cloned.1.call-start
  229.8 21.8 %reduce-scatter.6.cloned.1.call-done = bf16[256,2048]{1,0:T(8,128)(2,1)} async-done(((bf16[512,2048]{1,0:T(8,128)(2,1)}), bf16[256,2048]{1,0:T(8,128)(2,1)}) %reduce-scatter.6.cloned.1.call-update) | async-done | bytes 1048592 | tf_op jit(solution)/shard_map/reduce_scatter | solution.py:84
  251.6 0.0 reduce-scatter.4.cloned.1.call-start
  251.6 2.6 convolution_convert_fusion
  254.3 0.0 all-gather.15.cloned.1.call-start
  254.3 139.2 %reduce-scatter.8.cloned.1.call-done = bf16[8,2048]{1,0:T(8,128)(2,1)} async-done(((bf16[256,2048]{1,0:T(8,128)(2,1)}), bf16[8,2048]{1,0:T(8,128)(2,1)}) %reduce-scatter.8.cloned.1.call-update) | async-done | bytes 32784 | tf_op jit(solution)/shard_map/reduce_scatter | solution.py:85
  393.6 0.1 dynamic_update_slice.3
  393.7 100.6 %psum.7 = f32[5120]{0:T(1024)S(1)} all-reduce(f32[5120]{0:T(1024)S(1)} %pad_maximum_fusion.2), channel_id=1, replica_groups=mesh['dp_0'=16,'dp_1'=2,'fsdp_0'=4,'fsdp_1'=2,'fsdp_2'=2] {'dp_0','dp_1'..., use_global_device_ids=true, to_apply=%region_11.12 | all-reduce | flops 5120 | bytes 40960 | tf_op jit(solution)/shard_map/psum | solution.py:102
  494.2 0.6 slice.29
  494.8 0.6 dynamic_slice.3
  495.5 1.2 fusion.25
  496.7 1.9 fusion.23
  498.6 121.5 %all-gather.15.cloned.1.call-done = bf16[256,2048]{1,0:T(8,128)(2,1)} async-done(((bf16[8,2048]{1,0:T(8,128)(2,1)}), bf16[256,2048]{1,0:T(8,128)(2,1)}) %all-gather.15.cloned.1.call-update) | async-done | bytes 1048592 | tf_op jit(solution)/shard_map/all_gather | solution.py:86
  620.1 1.5 convert_element_type.58
  621.6 0.1 slice_bitcast_fusion
  621.7 1.3 copy.15
  623.0 1.1 slice.28
  (35 shorter events, 0.2 us)
Async XLA Ops:
  7.2 2.5 copy-start
  9.6 19.1 %copy-start.2 = (bf16[1024,256]{1,0:T(8,128)(2,1)S(1)}, bf16[1024,256]{1,0:T(8,128)(2,1)}, u32[]{:S(2)}) copy-start(bf16[1024,256]{1,0:T(8,128)(2,1)} %param.11) | copy-start | bytes 1572868
  12.1 50.1 %copy-start.3 = (f32[1024]{0:T(1024)S(1)}, f32[1024]{0:T(1024)}, u32[]{:S(2)}) copy-start(f32[1024]{0:T(1024)} %param.10) | copy-start | bytes 12292
  12.1 49.7 %all-to-all-start = ((bf16[32,4,2048]{2,1,0:T(4,128)(2,1)}), bf16[32,4,2048]{2,1,0:T(4,128)(2,1)S(1)}, u32[]{:S(2)}, u32[]{:S(2)}) async-start(bf16[32,4,2048]{2,1,0:T(4,128)(2,1)} %all_to_all.8), calls=%async_computation | async-start | bytes 1048576 | tf_op jit(solution)/shard_map/all_to_all | solution.py:20
  28.7 37.7 %all-gather.13.cloned.1.call-start = ((), (), s32[]{:S(2)}) async-start(), calls=%async_computation.7 | async-start | bytes 1572864 | tf_op jit(solution)/shard_map/all_gather | solution.py:52
  29.8 34.8 %copy-start.4 = (f32[256]{0:T(256)S(1)}, f32[256]{0:T(256)}, u32[]{:S(2)}) copy-start(f32[256]{0:T(256)} %param.12) | copy-start | bytes 3076
  29.8 98.1 %all-gather.11.cloned.1.call-start = ((), (), s32[]{:S(2)}) async-start(), calls=%async_computation.6 | async-start | bytes 2359296 | tf_op jit(solution)/shard_map/all_gather | solution.py:71
  63.2 138.0 %all-gather.7.cloned.1.call-start = ((), (), s32[]{:S(2)}) async-start(), calls=%async_computation.4 | async-start | bytes 2359296 | tf_op jit(solution)/shard_map/all_gather | solution.py:70
  64.0 157.8 %all-gather.9.cloned.1.call-start = ((), (), s32[]{:S(2)}) async-start(), calls=%async_computation.5 | async-start | bytes 1572864 | tf_op jit(solution)/shard_map/all_gather | solution.py:53
  64.5 187.0 %reduce-scatter.6.cloned.1.call-start = ((), (), s32[]{:S(2)}) async-start(), calls=%async_computation.9 | async-start | bytes 3145728 | tf_op jit(solution)/shard_map/reduce_scatter | solution.py:84
  204.7 22.2 %copy-start.6 = (bf16[1024,512]{0,1:T(8,128)(2,1)S(1)}, bf16[1024,512]{0,1:T(8,128)(2,1)}, u32[]{:S(2)}) copy-start(bf16[1024,512]{0,1:T(8,128)(2,1)} %all-gather.13.cloned.1.call-done) | copy-start | bytes 3145732
  221.8 5.1 copy-start.5
  226.9 1.3 copy-start.7
  229.7 21.9 %copy-start.8 = (bf16[1024,512]{1,0:T(8,128)(2,1)S(1)}, bf16[1024,512]{1,0:T(8,128)(2,1)}, u32[]{:S(2)}) copy-start(bf16[1024,512]{1,0:T(8,128)(2,1)} %copy-done.7) | copy-start | bytes 3145732
  229.7 163.8 %reduce-scatter.8.cloned.1.call-start = ((), (), s32[]{:S(2)}) async-start(), calls=%async_computation.10 | async-start | bytes 1081344 | tf_op jit(solution)/shard_map/reduce_scatter | solution.py:85
  251.6 243.9 %reduce-scatter.4.cloned.1.call-start = ((), (), s32[]{:S(2)}) async-start(), calls=%async_computation.8 | async-start | bytes 2359296 | tf_op jit(solution)/shard_map/reduce_scatter | solution.py:90
  254.3 365.9 %all-gather.15.cloned.1.call-start = ((), (), s32[]{:S(2)}) async-start(), calls=%async_computation.11 | async-start | bytes 1081344 | tf_op jit(solution)/shard_map/all_gather | solution.py:86
  621.6 1.4 copy-start.1
Sparse Core Ops, SparseCore 0:
  32.2 20.3 all-gather.12
  63.3 64.5 all-gather.10
  131.7 69.3 all-gather.6
  203.1 18.6 all-gather.8
  229.9 21.6 reduce-scatter.5
  254.2 139.2 reduce-scatter.7
  398.2 89.2 reduce-scatter.3
  489.5 130.5 all-gather.14
where the time goes:
time: 631 us
  waiting for transfers between devices  462 us (73%)
  blocking collectives  102 us (16%)
  matrix products  18.4 us (3%)
  starting transfers between devices  17 us (3%)
  between operations  14.4 us (2%)
  other arithmetic  9.85 us (2%)
  local copies, waits for them, and re-layouts  6.69 us (1%)
    reduce_scatter x1, waiting for transfers between devices, shards(): mine = lax.psum_scatter(mine, DP, scatter_dimension=0, tiled=True)  139 us
    all_gather x1, waiting for transfers between devices, shards(): whole = lax.all_gather(mine, DP, axis=0, tiled=True).astype(jnp.float32)  122 us
    psum x1, blocking collectives, shards(): lax.psum(jnp.concatenate([partial_gain_grad, wide.reshape(-1)]), DP_FSDP)  101 us
    all_gather x1, waiting for transfers between devices, shards(): all_cot = lax.all_gather(packed_cot, ROWS_AXES, axis=0, tiled=True)  68.8 us
    all_gather x1, waiting for transfers between devices, shards(): lax.all_gather(normed_local, ROWS_AXES, axis=0, tiled=True)  61.5 us
    all_to_all x1, waiting for transfers between devices, side_by_side(): lax.all_to_all(both, axis, split_axis=split_dim, concat_axis=concat_dim,...  31.9 us
    reduce_scatter x1, waiting for transfers between devices, shards(): mine = lax.psum_scatter(parts, 'fsdp_2', scatter_dimension=0, tiled=True)  21.8 us
    all_gather x1, waiting for transfers between devices, shards(): down_weight = lax.all_gather(down_weight, 'fsdp_2', axis=0, tiled=True)  17 us
  transfers between devices with their start and end apart: 9, of which 7 were waited for; matrix products, arithmetic and copies ran while one was open for 3% of the time, Pallas kernels for 0%

commit v1 on v0

v1 whole, which is shorter than its diff:
```python
import jax
import jax.numpy as jnp
from jax import lax
from jax.experimental import pallas as pl
from jax.experimental.pallas import tpu as pltpu
from jax.sharding import Mesh
from jax.sharding import PartitionSpec as P

FSDP = ("fsdp_0", "fsdp_1", "fsdp_2")
DP_FSDP = ("dp_0", "dp_1", "fsdp_0", "fsdp_1", "fsdp_2")
MESH = pl.DeviceIdType.MESH

root_two_pi = 0.7978845608
cubic = 0.044715

NZ, NX = 16, 4
OFFSETS = [0, 1, 15, 2, 14, 3, 13, 4, 12, 5, 11, 6, 10, 7, 9, 8]
CHUNKS = 4
F32, BF16 = jnp.float32, jnp.bfloat16


def gelu_pair(pre):
    inner = root_two_pi * (pre + cubic * pre * pre * pre)
    tangent = jnp.tanh(inner)
    act = 0.5 * pre * (1.0 + tangent)
    slope = 0.5 * (1.0 + tangent) + 0.5 * pre * (1.0 - tangent * tangent) * root_two_pi * (
        1.0 + 3.0 * cubic * pre * pre
    )
    return (act, slope)


def nn(a, b):
    return lax.dot_general(a, b, (((1,), (0,)), ((), ())), preferred_element_type=F32)


def nt(a, b):
    return lax.dot_general(a, b, (((1,), (1,)), ((), ())), preferred_element_type=F32)


def tn(a, b):
    return lax.dot_general(a, b, (((0,), (0,)), ((), ())), preferred_element_type=F32)


def iota(shape, dim):
    return lax.broadcasted_iota(jnp.int32, shape, dim)


def kernel(
    tok, cot, routes, gain, wu_in, bu_in, wd_in,
    dx_out, up_out, down_out, bias_out, gain_out,
    send, land, g, wu, wd, bu, acc, bacc, part, ret, xh, rs, dxs,
    cs, cr, sp, rp, sm, rm, ys, yr, ag,
    small_s, small_r, gs, ar, bs, br, cc_s, cr_r,
    a2a_s, a2a_r, gat_s, gat_r, w_s, w_r, p_s, p_r, cs_s, cs_r,
    rp_s, rp_r, rm_s, rm_r, y_s, y_r, ap_s, ap_r, am_s, am_r,
    sm_s, sm_r, ga_s, ga_r, gb_s, gb_r, gc_s, gc_r,
):
    z, yl = lax.axis_index("dp_0"), lax.axis_index("dp_1")
    x, yh, c = lax.axis_index("fsdp_0"), lax.axis_index("fsdp_1"), lax.axis_index("fsdp_2")
    pending = []

    def zpeer(dz, dy):
        return (lax.rem(z + dz, NZ), (yl + dy) % 2, x, yh, c)

    def xpeer(rx, ry):
        return (z, yl, lax.rem(x + rx, NX), (yh + ry) % 2, c)

    sibling = (z, yl, x, yh, 1 - c)

    def remote(src, dst, ssem, rsem, peer):
        return pltpu.make_async_remote_copy(
            src_ref=src, dst_ref=dst, send_sem=ssem, recv_sem=rsem,
            device_id=peer, device_id_type=MESH,
        )

    def go(copy):
        copy.start()
        pending.append(copy)
        return copy

    barrier = pltpu.get_barrier_semaphore()
    peers = [zpeer(dz, dy) for dz in range(NZ) for dy in range(2) if dz or dy]
    peers += [xpeer(rx, ry) for rx in range(NX) for ry in range(2) if rx or ry]
    peers.append(sibling)
    for peer in peers:
        pl.semaphore_signal(barrier, inc=1, device_id=peer, device_id_type=MESH)

    target = routes[...]
    hot = (iota((40, 128), 0) == target).astype(BF16)
    before = (iota((128, 128), 0) < iota((128, 128), 1)).astype(BF16)
    ranked = jnp.sum(nn(hot, before) * hot.astype(F32), axis=0, keepdims=True).astype(jnp.int32)
    dz = ((target >> 1) - z + NZ) & (NZ - 1)
    pos = jnp.where(dz == 0, 0, jnp.where(dz <= NZ // 2, 2 * dz - 1, 2 * (NZ - dz)))
    dy = ((target & 1) + yl) & 1
    row = jnp.where(target < 2 * NZ, (pos * 2 + dy) * 8 + ranked, -8)
    line = iota((256, 128), 0)
    placed = nn((line == row).astype(BF16), tok[...]) + nn(
        (line == row + 4).astype(BF16), cot[...]
    )
    send[...] = placed.astype(BF16).reshape(32, 8, 1024)
    land[0] = send[0]
    wu[0:256] = wu_in[...]
    wd[0:256] = wd_in[...]
    bu[0] = bu_in[...]

    pl.semaphore_wait(barrier, len(peers))

    a2a = {}
    for t in range(1, 32):
        a2a[t] = go(
            remote(send.at[t], land.at[t], a2a_s.at[t], a2a_r.at[t], zpeer(OFFSETS[t // 2], t % 2))
        )
    weights = [
        go(remote(wu_in, wu.at[256:512], w_s.at[0], w_r.at[0], sibling)),
        go(remote(wd_in, wd.at[256:512], w_s.at[1], w_r.at[1], sibling)),
        go(remote(bu_in, bu.at[1], w_s.at[2], w_r.at[2], sibling)),
    ]

    moves = [
        (0, 1, (0, 1)),
        (0, 6, (1, 0)), (0, 2, (3, 0)),
        (1, 7, (1, 0)), (1, 3, (3, 0)),
        (6, 4, (1, 0)), (3, 5, (3, 0)),
    ]

    def move(k, i):
        src, dst, (rx, ry) = moves[i]
        return remote(
            g.at[k, :, src], g.at[k, :, dst], gat_s.at[k, i], gat_r.at[k, i], xpeer(rx, ry)
        )

    sorter = iota((64, 64), 0)
    column = iota((64, 64), 1)
    wanted = (column // 8) * 4 + (column % 4) + jnp.where(column % 8 >= 4, 32, 0)
    sort = (sorter == wanted).astype(BF16)

    def own(k):
        for t in range(8 * k, 8 * k + 8):
            if t:
                a2a[t].wait_recv()
        rows = nn(sort, land[8 * k : 8 * k + 8].reshape(64, 1024))
        values = rows[0:32]
        centered = values - jnp.mean(values, axis=1, keepdims=True)
        variance = jnp.mean(centered * centered, axis=1, keepdims=True)
        inverse = 1.0 / jnp.sqrt(variance + 1e-05)
        standard = centered * inverse
        xh[k] = standard
        rs[k] = jnp.broadcast_to(inverse, (32, 128))
        g[k, 0, 0] = (standard * gain[...]).astype(BF16)
        g[k, 1, 0] = rows[32:64].astype(BF16)
        for i in range(3):
            go(move(k, i))

    def second(k):
        move(k, 0).wait_recv()
        go(move(k, 3))
        go(move(k, 4))

    def third(k):
        move(k, 1).wait_recv()
        go(move(k, 5))
        move(k, 4).wait_recv()
        go(move(k, 6))

    def compute(k):
        for i in (2, 3, 5, 6):
            move(k, i).wait_recv()
        normed = g[k, 0].reshape(256, 1024)
        outer = g[k, 1].reshape(256, 1024)
        bias = jnp.concatenate([bu[0], bu[1]], axis=1)
        act, slope = gelu_pair(nt(normed, wu[...]) + bias)
        pre_grad = (nt(outer, wd[...]) * slope).astype(BF16)
        act = act.astype(BF16)
        up = tn(pre_grad, normed).reshape(2, 16, 16, 1024)
        down = tn(act, outer).reshape(2, 16, 16, 1024)
        biases = jnp.sum(pre_grad.astype(F32), axis=0, keepdims=True)
        if k == 0:
            acc[:, 0:16] = up
            acc[:, 16:32] = down
            bacc[...] = biases
        else:
            acc[:, 0:16] += up
            acc[:, 16:32] += down
            bacc[...] += biases
        part[k] = nn(pre_grad, wu[...]).astype(BF16).reshape(8, 32, 1024)

    own(0)
    own(1)
    second(0)
    third(0)
    second(1)
    own(2)
    third(1)
    for w in weights:
        w.wait_recv()
    compute(0)
    second(2)
    own(3)
    third(2)
    compute(1)
    second(3)
    third(3)
    compute(2)
    compute(3)

    def across(r, h):
        return remote(cs.at[r, h], cr.at[r, h], cs_s.at[r, h], cs_r.at[r, h], sibling)

    for r in (8, 9, 7, 10, 6, 11, 5, 12, 4, 13, 3, 14, 2, 15, 1, 0):
        o = lax.rem(z + r, NZ)
        for h in range(2):
            cs[r, h] = acc[1, 2 * o + h].astype(BF16)
            go(across(r, h))

    def home(m):
        rx, ry = m // 2, m % 2
        there = ((NX - rx) % NX) * 2 + ry
        return remote(part.at[:, m], ret.at[there], p_s.at[m], p_r.at[there], xpeer(rx, ry))

    for m in (1, 2, 6, 3, 7, 4, 5):
        go(home(m))

    def mine(r, h):
        return acc[0, 2 * lax.rem(z + r, NZ) + h] + cr[r, h].astype(F32)

    def plus(s, h):
        return remote(sp.at[s, h], rp.at[s, h], rp_s.at[s, h], rp_r.at[s, h], zpeer(1, 0))

    def minus(s, h):
        return remote(sm.at[s, h], rm.at[s, h], rm_s.at[s, h], rm_r.at[s, h], zpeer(NZ - 1, 0))

    def ring(s):
        for h in range(2):
            across(8 - s, h).wait_recv()
            value = mine(8 - s, h)
            if s:
                plus(s - 1, h).wait_recv()
                value = value + rp[s - 1, h].astype(F32)
            sp[s, h] = value.astype(BF16)
            go(plus(s, h))
            if s < 7:
                across(9 + s, h).wait_recv()
                value = mine(9 + s, h)
                if s:
                    minus(s - 1, h).wait_recv()
                    value = value + rm[s - 1, h].astype(F32)
                sm[s, h] = value.astype(BF16)
                go(minus(s, h))

    ring(0)
    weighted = jnp.zeros((1, 1024), F32)
    for half in range(2):
        prod = acc[half, 0:16].reshape(256, 1024) * wu[256 * half : 256 * half + 256].astype(F32)
        weighted = weighted + jnp.sum(prod, axis=0, keepdims=True)
    weighted = weighted / gain[...]
    small_s[:, 0:1024] = weighted
    small_s[:, 1024:1280] = bacc[:, 256:512]
    to_sibling = go(remote(small_s, small_r, sm_s.at[0], sm_r.at[0], sibling))
    ring(1)
    to_sibling.wait_recv()
    whole_gain = weighted + small_r[:, 0:1024]
    for j in range(8):
        gs[j] = whole_gain[:, 128 * j : 128 * j + 128]
    bs[:, 128:384] = bacc[:, 0:256] + small_r[:, 1024:1280]
    here = x * 2 + yh

    def there_of(m):
        return lax.rem(x + m // 2, NX) * 2 + (yh + m % 2) % 2

    ar[here] = gs[here]
    for m in range(1, 8):
        go(
            remote(
                gs.at[there_of(m)], ar.at[here], ga_s.at[m], ga_r.at[here], xpeer(m // 2, m % 2)
            )
        )
    ring(2)
    ring(3)
    for m in range(1, 8):
        j = there_of(m)
        remote(gs.at[j], ar.at[j], ga_s.at[m], ga_r.at[j], sibling).wait_recv()
    bs[:, 0:128] = jnp.sum(ar[...], axis=0)
    number = z * 2 + yl
    br[number] = bs[...]
    for t in range(1, 32):
        go(
            remote(
                bs, br.at[number], gb_s.at[t], gb_r.at[number], zpeer(OFFSETS[t // 2], t % 2)
            )
        )
    for s in range(4, 8):
        ring(s)

    def swap(h):
        return remote(ys.at[h], yr.at[h], y_s.at[h], y_r.at[h], zpeer(0, 1))

    for h in range(2):
        across(0, h).wait_recv()
        plus(7, h).wait_recv()
        minus(6, h).wait_recv()
        total = mine(0, h) + rp[7, h].astype(F32) + rm[6, h].astype(F32)
        ys[h] = total.astype(BF16)
        go(swap(h))

    def spread(s, h, sign):
        origin = lax.rem(z + NZ - sign * s, NZ)
        spot = ag.at[2 * origin + h]
        if sign > 0:
            return remote(spot, spot, ap_s.at[s, h], ap_r.at[s, h], zpeer(1, 0))
        return remote(spot, spot, am_s.at[s, h], am_r.at[s, h], zpeer(NZ - 1, 0))

    def arrived(s, h, sign):
        origin = lax.rem(z + NZ - sign * (s + 1), NZ)
        spot = ag.at[2 * origin + h]
        if sign > 0:
            return remote(spot, spot, ap_s.at[s, h], ap_r.at[s, h], zpeer(1, 0))
        return remote(spot, spot, am_s.at[s, h], am_r.at[s, h], zpeer(NZ - 1, 0))

    for h in range(2):
        swap(h).wait_recv()
        ag[2 * z + h] = (ys[h].astype(F32) + yr[h].astype(F32)).astype(BF16)
        go(spread(0, h, 1))
        go(spread(0, h, -1))

    def turn(s):
        for h in range(2):
            for sign in (1, -1):
                if sign > 0 or s < 8:
                    arrived(s - 1, h, sign).wait_recv()
                    if s < (8 if sign > 0 else 7):
                        go(spread(s, h, sign))

    turn(1)
    for t in range(1, 32):
        source = lax.rem(z + OFFSETS[t // 2], NZ) * 2 + (yl + t % 2) % 2
        remote(bs, br.at[source], gb_s.at[t], gb_r.at[source], sibling).wait_recv()
    sums = jnp.sum(br[...], axis=0)
    bias_out[...] = sums[:, 128:384]
    cc_s[...] = sums[:, 0:128]
    cr_r[here] = sums[:, 0:128]
    for m in range(1, 8):
        go(remote(cc_s, cr_r.at[here], gc_s.at[m], gc_r.at[here], xpeer(m // 2, m % 2)))
    for s in range(2, 5):
        turn(s)

    for m in range(1, 8):
        remote(part.at[:, m], ret.at[m], p_s.at[m], p_r.at[m], sibling).wait_recv()
    for k in range(CHUNKS):
        summed = part[k, 0].astype(F32)
        for m in range(1, 8):
            summed = summed + ret[m, k].astype(F32)
        scaled = summed * gain[...]
        standard = xh[k]
        first = jnp.mean(scaled, axis=1, keepdims=True)
        cross = jnp.mean(scaled * standard, axis=1, keepdims=True)
        value = g[k, 1, 0].astype(F32) + rs[k][:, 0:1] * (scaled - first - standard * cross)
        dxs[k] = value.astype(BF16)
        turn(5 + k)

    spot = iota((128, 128), 1)
    tile = spot // 4
    at = tile // 2
    offset = jnp.where(at == 0, 0, jnp.where(at % 2 == 1, (at + 1) // 2, NZ - at // 2))
    source = ((z - offset + NZ) & (NZ - 1)) * 2 + (((tile % 2) + yl) & 1)
    perm = (iota((128, 128), 0) == source * 4 + spot % 4).astype(BF16)
    dx_out[...] = nn(perm, dxs[...].reshape(128, 1024)).astype(BF16)
    up_out[...] = ag[0:16].reshape(256, 1024)
    down_out[...] = ag[16:32].reshape(256, 1024)
    for m in range(1, 8):
        j = there_of(m)
        remote(cc_s, cr_r.at[j], gc_s.at[m], gc_r.at[j], sibling).wait_recv()
    gain_out[...] = cr_r[...].reshape(8, 128)
    for copy in pending:
        copy.wait_send()


def shards(tokens, cotangent, routes, norm_gain_vector, up_weight, up_bias, down_weight):
    vmem, sem = pltpu.VMEM, pltpu.SemaphoreType.DMA
    dx, up, down, bias, gain = pl.pallas_call(
        kernel,
        out_shape=(
            jax.ShapeDtypeStruct((128, 1024), BF16),
            jax.ShapeDtypeStruct((256, 1024), BF16),
            jax.ShapeDtypeStruct((256, 1024), BF16),
            jax.ShapeDtypeStruct((1, 256), F32),
            jax.ShapeDtypeStruct((8, 128), F32),
        ),
        in_specs=[pl.BlockSpec(memory_space=pltpu.VMEM)] * 7,
        out_specs=[pl.BlockSpec(memory_space=pltpu.VMEM)] * 5,
        scratch_shapes=[
            vmem((32, 8, 1024), BF16),
            vmem((32, 8, 1024), BF16),
            vmem((CHUNKS, 2, 8, 32, 1024), BF16),
            vmem((512, 1024), BF16),
            vmem((512, 1024), BF16),
            vmem((2, 1, 256), F32),
            vmem((2, 32, 16, 1024), F32),
            vmem((1, 512), F32),
            vmem((CHUNKS, 8, 32, 1024), BF16),
            vmem((8, CHUNKS, 32, 1024), BF16),
            vmem((CHUNKS, 32, 1024), F32),
            vmem((CHUNKS, 32, 128), F32),
            vmem((CHUNKS, 32, 1024), BF16),
            vmem((16, 2, 16, 1024), BF16),
            vmem((16, 2, 16, 1024), BF16),
            vmem((8, 2, 16, 1024), BF16),
            vmem((8, 2, 16, 1024), BF16),
            vmem((8, 2, 16, 1024), BF16),
            vmem((8, 2, 16, 1024), BF16),
            vmem((2, 16, 1024), BF16),
            vmem((2, 16, 1024), BF16),
            vmem((32, 16, 1024), BF16),
            vmem((1, 1280), F32),
            vmem((1, 1280), F32),
            vmem((8, 1, 128), F32),
            vmem((8, 1, 128), F32),
            vmem((1, 384), F32),
            vmem((32, 1, 384), F32),
            vmem((1, 128), F32),
            vmem((8, 1, 128), F32),
            sem((32,)), sem((32,)),
            sem((CHUNKS, 7)), sem((CHUNKS, 7)),
            sem((3,)), sem((3,)),
            sem((8,)), sem((8,)),
            sem((16, 2)), sem((16, 2)),
            sem((8, 2)), sem((8, 2)), sem((8, 2)), sem((8, 2)),
            sem((2,)), sem((2,)),
            sem((8, 2)), sem((8, 2)), sem((8, 2)), sem((8, 2)),
            sem((1,)), sem((1,)),
            sem((8,)), sem((8,)),
            sem((32,)), sem((32,)),
            sem((8,)), sem((8,)),
        ],
        compiler_params=pltpu.CompilerParams(
            collective_id=0, has_side_effects=True, vmem_limit_bytes=60 * 1024 * 1024
        ),
        name="ffn_backward",
    )(
        tokens,
        cotangent,
        routes.reshape(1, -1),
        norm_gain_vector.reshape(1, -1),
        up_weight.T,
        up_bias.reshape(1, -1),
        down_weight,
    )
    return (
        dx,
        up.T.astype(F32),
        bias.reshape(-1),
        down.astype(F32),
        gain.reshape(-1),
    )


def solution(mesh):
    finer = Mesh(mesh.devices.reshape(NZ, 2, NX, 2, 2), DP_FSDP)
    return jax.shard_map(
        shards,
        mesh=finer,
        in_specs=(
            P(DP_FSDP, None),
            P(DP_FSDP, None),
            P(DP_FSDP, None),
            P(),
            P(None, FSDP),
            P(FSDP),
            P(FSDP, None),
        ),
        out_specs=(P(DP_FSDP, None), P(None, FSDP), P(FSDP), P(FSDP, None), P()),
        check_vma=False,
    )
```

time: 631 us -> 147 us (0.23)
  the two profiles are of different devices: /device:TPU:2 before, /device:TPU:18 now
where the time goes in v1:
time: 147 us
  Pallas kernels  139 us (95%)
  local copies, waits for them, and re-layouts  5.22 us (4%)
  other arithmetic  2.23 us (2%)
    pallas_call x1, Pallas kernels, shards(): pl.pallas_call(kernel, out_shape=(jax.ShapeDtypeStruct((128, 1024), BF16)...  139 us
    unnamed x13, local copies, waits for them, and re-layouts  5.22 us

profile of v1, /device:TPU:18, one launch (start us, length us, event | category | flops | bytes accessed | tf_op | source)
XLA Modules:
  0.0 147.2 jit_solution(11084490503274528554)
XLA Ops:
  0.6 2.0 %copy.12 = bf16[1024,256]{0,1:T(8,128)(2,1)} copy(bf16[1024,256]{1,0:T(8,128)(2,1)} %param.11) | data formatting | bytes 1048576 | tf_op args[4]
  2.7 139.0 %ffn_backward.1 = (bf16[128,1024]{1,0:T(8,128)(2,1)}, bf16[256,1024]{1,0:T(8,128)(2,1)}, bf16[256,1024]{1,0:T(8,128)(2,1)}, f32[1,256]{1,0:T(1,128)}, f32[8,128]{1,0:T(8,128)}) custom-call(bf16[128,1024]{1,0:T(8,128)(2,1)} %tok.1, bf16[128,1024]{1,0:T(8,128)(2,1)} %cot.1, s32[1,128]{1,0:T(1,128)} %bitcast.13, f32[1,1024]{1,0:T(1,128)} %bitcast.9, ...), custom_call_target="tpu_custom_call" | custom-call | tf_op jit(solution)/shard_map/ffn_backward/pallas_call | solution.py:379
  141.7 1.1 convert_bitcast_fusion
  142.9 0.0 copy-start
  142.9 1.3 copy.13
  144.2 0.0 copy-done
  144.2 0.0 copy-start.1
  144.2 1.1 convert_element_type.11
  145.3 0.0 copy-done.1
  145.3 0.0 copy-start.3
  145.3 0.0 copy-start.2
  145.3 0.7 copy.17
  146.0 0.0 copy-done.3
  146.0 0.6 copy.18
  146.6 0.0 copy-done.2
  146.6 0.6 copy.19
Async XLA Ops:
  142.9 1.3 copy-start
  144.2 1.1 copy-start.1
  145.3 0.7 copy-start.3
  145.3 1.3 copy-start.2

commit v2 on v1

--- a/solution.py
+++ b/solution.py
@@ -15,7 +15,7 @@
 
 NZ, NX = 16, 4
 OFFSETS = [0, 1, 15, 2, 14, 3, 13, 4, 12, 5, 11, 6, 10, 7, 9, 8]
-CHUNKS = 4
+CHUNKS, SUBS = 8, 4
 F32, BF16 = jnp.float32, jnp.bfloat16
 
 
@@ -47,8 +47,8 @@
 
 def kernel(
     tok, cot, routes, gain, wu_in, bu_in, wd_in,
-    dx_out, up_out, down_out, bias_out, gain_out,
-    send, land, g, wu, wd, bu, acc, bacc, part, ret, xh, rs, dxs,
+    dxs, ag_out, bias_out, gain_out,
+    send, land, g, wu, wd, bu, acc, bacc, part, fars, near_s, near_r, ysend, yrecv, xh, rs,
     cs, cr, sp, rp, sm, rm, ys, yr, ag,
     small_s, small_r, gs, ar, bs, br, cc_s, cr_r,
     a2a_s, a2a_r, gat_s, gat_r, w_s, w_r, p_s, p_r, cs_s, cs_r,
@@ -99,7 +99,6 @@
     )
     send[...] = placed.astype(BF16).reshape(32, 8, 1024)
     land[0] = send[0]
-    wu[0:256] = wu_in[...]
     wd[0:256] = wd_in[...]
     bu[0] = bu_in[...]
 
@@ -110,8 +109,9 @@
         a2a[t] = go(
             remote(send.at[t], land.at[t], a2a_s.at[t], a2a_r.at[t], zpeer(OFFSETS[t // 2], t % 2))
         )
+    wu[0:256] = wu_in[...].T
     weights = [
-        go(remote(wu_in, wu.at[256:512], w_s.at[0], w_r.at[0], sibling)),
+        go(remote(wu.at[0:256], wu.at[256:512], w_s.at[0], w_r.at[0], sibling)),
         go(remote(wd_in, wd.at[256:512], w_s.at[1], w_r.at[1], sibling)),
         go(remote(bu_in, bu.at[1], w_s.at[2], w_r.at[2], sibling)),
     ]
@@ -129,25 +129,25 @@
             g.at[k, :, src], g.at[k, :, dst], gat_s.at[k, i], gat_r.at[k, i], xpeer(rx, ry)
         )
 
-    sorter = iota((64, 64), 0)
-    column = iota((64, 64), 1)
-    wanted = (column // 8) * 4 + (column % 4) + jnp.where(column % 8 >= 4, 32, 0)
+    sorter = iota((32, 32), 0)
+    column = iota((32, 32), 1)
+    wanted = (column // 8) * 4 + (column % 4) + jnp.where(column % 8 >= 4, 16, 0)
     sort = (sorter == wanted).astype(BF16)
 
     def own(k):
-        for t in range(8 * k, 8 * k + 8):
+        for t in range(4 * k, 4 * k + 4):
             if t:
                 a2a[t].wait_recv()
-        rows = nn(sort, land[8 * k : 8 * k + 8].reshape(64, 1024))
-        values = rows[0:32]
+        rows = nn(sort, land[4 * k : 4 * k + 4].reshape(32, 1024))
+        values = rows[0:16]
         centered = values - jnp.mean(values, axis=1, keepdims=True)
         variance = jnp.mean(centered * centered, axis=1, keepdims=True)
         inverse = 1.0 / jnp.sqrt(variance + 1e-05)
         standard = centered * inverse
         xh[k] = standard
-        rs[k] = jnp.broadcast_to(inverse, (32, 128))
+        rs[k] = jnp.broadcast_to(inverse, (16, 128))
         g[k, 0, 0] = (standard * gain[...]).astype(BF16)
-        g[k, 1, 0] = rows[32:64].astype(BF16)
+        g[k, 1, 0] = rows[16:32].astype(BF16)
         for i in range(3):
             go(move(k, i))
 
@@ -162,66 +162,115 @@
         move(k, 4).wait_recv()
         go(move(k, 6))
 
-    def compute(k):
-        for i in (2, 3, 5, 6):
-            move(k, i).wait_recv()
-        normed = g[k, 0].reshape(256, 1024)
-        outer = g[k, 1].reshape(256, 1024)
+    def compute(j, n):
+        for k in range(j, j + n):
+            for i in (2, 3, 5, 6):
+                move(k, i).wait_recv()
+        normed = g[j : j + n, 0].reshape(128 * n, 1024)
+        outer = g[j : j + n, 1].reshape(128 * n, 1024)
         bias = jnp.concatenate([bu[0], bu[1]], axis=1)
         act, slope = gelu_pair(nt(normed, wu[...]) + bias)
         pre_grad = (nt(outer, wd[...]) * slope).astype(BF16)
         act = act.astype(BF16)
-        up = tn(pre_grad, normed).reshape(2, 16, 16, 1024)
-        down = tn(act, outer).reshape(2, 16, 16, 1024)
+        up = tn(pre_grad, normed).reshape(2, 32, 8, 1024)
+        down = tn(act, outer).reshape(2, 32, 8, 1024)
         biases = jnp.sum(pre_grad.astype(F32), axis=0, keepdims=True)
-        if k == 0:
-            acc[:, 0:16] = up
-            acc[:, 16:32] = down
+        if j == 0:
+            acc[:, 0:32] = up
+            acc[:, 32:64] = down
             bacc[...] = biases
         else:
-            acc[:, 0:16] += up
-            acc[:, 16:32] += down
+            acc[:, 0:32] += up
+            acc[:, 32:64] += down
             bacc[...] += biases
-        part[k] = nn(pre_grad, wu[...]).astype(BF16).reshape(8, 32, 1024)
+        part[j : j + n] = nn(pre_grad, wu[...]).astype(BF16).reshape(n, 8, 16, 1024)
 
     own(0)
     own(1)
+    own(2)
     second(0)
+    own(3)
+    second(1)
     third(0)
-    second(1)
-    own(2)
+    second(2)
     third(1)
+    own(4)
+    second(3)
+    third(2)
     for w in weights:
         w.wait_recv()
-    compute(0)
-    second(2)
-    own(3)
-    third(2)
-    compute(1)
-    second(3)
+    compute(0, 2)
+    own(5)
     third(3)
-    compute(2)
-    compute(3)
-
-    def across(r, h):
-        return remote(cs.at[r, h], cr.at[r, h], cs_s.at[r, h], cs_r.at[r, h], sibling)
+    second(4)
+    third(4)
+    compute(2, 2)
+    own(6)
+    second(5)
+    third(5)
+    second(6)
+    own(7)
+    compute(4, 2)
+    third(6)
+    second(7)
+    third(7)
+    compute(6, 2)
+
+    def across(r):
+        return remote(cs.at[r], cr.at[r], cs_s.at[r], cs_r.at[r], sibling)
 
     for r in (8, 9, 7, 10, 6, 11, 5, 12, 4, 13, 3, 14, 2, 15, 1, 0):
         o = lax.rem(z + r, NZ)
-        for h in range(2):
-            cs[r, h] = acc[1, 2 * o + h].astype(BF16)
-            go(across(r, h))
-
-    def home(m):
-        rx, ry = m // 2, m % 2
-        there = ((NX - rx) % NX) * 2 + ry
-        return remote(part.at[:, m], ret.at[there], p_s.at[m], p_r.at[there], xpeer(rx, ry))
-
-    for m in (1, 2, 6, 3, 7, 4, 5):
-        go(home(m))
+        cs[r] = acc[1, pl.ds(o * SUBS, SUBS)].astype(BF16)
+        go(across(r))
+
+    right, left = xpeer(1, 0), xpeer(NX - 1, 0)
+    lo, hi = pl.ds(0, 4), pl.ds(4, 4)
+
+    def raw_plus():
+        return remote(part.at[hi, 2:4], near_r.at[0, hi], p_s.at[2], p_r.at[2], right)
+
+    def raw_minus():
+        return remote(part.at[lo, 6:8], near_r.at[1, lo], p_s.at[3], p_r.at[3], left)
+
+    def far_plus():
+        return remote(part.at[lo, 4:6], fars.at[0], p_s.at[0], p_r.at[0], right)
+
+    def far_minus():
+        return remote(part.at[hi, 4:6], fars.at[1], p_s.at[1], p_r.at[1], left)
+
+    def sum_plus():
+        return remote(near_s.at[0], near_r.at[0, lo], p_s.at[4], p_r.at[4], right)
+
+    def sum_minus():
+        return remote(near_s.at[1], near_r.at[1, hi], p_s.at[5], p_r.at[5], left)
+
+    def last_leg():
+        return remote(ysend, yrecv, p_s.at[6], p_r.at[6], xpeer(0, 1))
+
+    for copy in (far_plus(), far_minus(), raw_plus(), raw_minus()):
+        go(copy)
+
+    def along_plus():
+        far_plus().wait_recv()
+        near_s[0] = (part[0:4, 2:4].astype(F32) + fars[0].astype(F32)).astype(BF16)
+        go(sum_plus())
+
+    def along_minus():
+        far_minus().wait_recv()
+        near_s[1] = (part[4:8, 6:8].astype(F32) + fars[1].astype(F32)).astype(BF16)
+        go(sum_minus())
+
+    def across_y():
+        for copy in (raw_plus(), raw_minus(), sum_plus(), sum_minus()):
+            copy.wait_recv()
+        ysend[...] = (
+            part[:, 1].astype(F32) + near_r[0, :, 1].astype(F32) + near_r[1, :, 1].astype(F32)
+        ).astype(BF16)
+        go(last_leg())
 
     def mine(r, h):
-        return acc[0, 2 * lax.rem(z + r, NZ) + h] + cr[r, h].astype(F32)
+        return acc[0, SUBS * lax.rem(z + r, NZ) + h] + cr[r, h].astype(F32)
 
     def plus(s, h):
         return remote(sp.at[s, h], rp.at[s, h], rp_s.at[s, h], rp_r.at[s, h], zpeer(1, 0))
@@ -230,8 +279,10 @@
         return remote(sm.at[s, h], rm.at[s, h], rm_s.at[s, h], rm_r.at[s, h], zpeer(NZ - 1, 0))
 
     def ring(s):
-        for h in range(2):
-            across(8 - s, h).wait_recv()
+        across(8 - s).wait_recv()
+        if s < 7:
+            across(9 + s).wait_recv()
+        for h in range(SUBS):
             value = mine(8 - s, h)
             if s:
                 plus(s - 1, h).wait_recv()
@@ -239,7 +290,6 @@
             sp[s, h] = value.astype(BF16)
             go(plus(s, h))
             if s < 7:
-                across(9 + s, h).wait_recv()
                 value = mine(9 + s, h)
                 if s:
                     minus(s - 1, h).wait_recv()
@@ -250,7 +300,7 @@
     ring(0)
     weighted = jnp.zeros((1, 1024), F32)
     for half in range(2):
-        prod = acc[half, 0:16].reshape(256, 1024) * wu[256 * half : 256 * half + 256].astype(F32)
+        prod = acc[half, 0:32].reshape(256, 1024) * wu[256 * half : 256 * half + 256].astype(F32)
         weighted = weighted + jnp.sum(prod, axis=0, keepdims=True)
     weighted = weighted / gain[...]
     small_s[:, 0:1024] = weighted
@@ -276,6 +326,9 @@
         )
     ring(2)
     ring(3)
+    along_plus()
+    ring(4)
+    along_minus()
     for m in range(1, 8):
         j = there_of(m)
         remote(gs.at[j], ar.at[j], ga_s.at[m], ga_r.at[j], sibling).wait_recv()
@@ -288,42 +341,43 @@
                 bs, br.at[number], gb_s.at[t], gb_r.at[number], zpeer(OFFSETS[t // 2], t % 2)
             )
         )
-    for s in range(4, 8):
+    for s in range(5, 8):
         ring(s)
 
     def swap(h):
         return remote(ys.at[h], yr.at[h], y_s.at[h], y_r.at[h], zpeer(0, 1))
 
-    for h in range(2):
-        across(0, h).wait_recv()
+    across(0).wait_recv()
+    for h in range(SUBS):
         plus(7, h).wait_recv()
         minus(6, h).wait_recv()
         total = mine(0, h) + rp[7, h].astype(F32) + rm[6, h].astype(F32)
         ys[h] = total.astype(BF16)
         go(swap(h))
+    across_y()
 
     def spread(s, h, sign):
         origin = lax.rem(z + NZ - sign * s, NZ)
-        spot = ag.at[2 * origin + h]
+        spot = ag.at[SUBS * origin + h]
         if sign > 0:
             return remote(spot, spot, ap_s.at[s, h], ap_r.at[s, h], zpeer(1, 0))
         return remote(spot, spot, am_s.at[s, h], am_r.at[s, h], zpeer(NZ - 1, 0))
 
     def arrived(s, h, sign):
         origin = lax.rem(z + NZ - sign * (s + 1), NZ)
-        spot = ag.at[2 * origin + h]
+        spot = ag.at[SUBS * origin + h]
         if sign > 0:
             return remote(spot, spot, ap_s.at[s, h], ap_r.at[s, h], zpeer(1, 0))
         return remote(spot, spot, am_s.at[s, h], am_r.at[s, h], zpeer(NZ - 1, 0))
 
-    for h in range(2):
+    for h in range(SUBS):
         swap(h).wait_recv()
-        ag[2 * z + h] = (ys[h].astype(F32) + yr[h].astype(F32)).astype(BF16)
+        ag[SUBS * z + h] = (ys[h].astype(F32) + yr[h].astype(F32)).astype(BF16)
         go(spread(0, h, 1))
         go(spread(0, h, -1))
 
     def turn(s):
-        for h in range(2):
+        for h in range(SUBS):
             for sign in (1, -1):
                 if sign > 0 or s < 8:
                     arrived(s - 1, h, sign).wait_recv()
@@ -343,20 +397,36 @@
     for s in range(2, 5):
         turn(s)
 
-    for m in range(1, 8):
-        remote(part.at[:, m], ret.at[m], p_s.at[m], p_r.at[m], sibling).wait_recv()
-    for k in range(CHUNKS):
-        summed = part[k, 0].astype(F32)
-        for m in range(1, 8):
-            summed = summed + ret[m, k].astype(F32)
+    last_leg().wait_recv()
+    for i in range(4):
+        k = pl.ds(2 * i, 2)
+        summed = (
+            part[k, 0].astype(F32)
+            + near_r[0, k, 0].astype(F32)
+            + near_r[1, k, 0].astype(F32)
+            + yrecv[k].astype(F32)
+        ).reshape(32, 1024)
         scaled = summed * gain[...]
-        standard = xh[k]
+        standard = xh[k].reshape(32, 1024)
         first = jnp.mean(scaled, axis=1, keepdims=True)
         cross = jnp.mean(scaled * standard, axis=1, keepdims=True)
-        value = g[k, 1, 0].astype(F32) + rs[k][:, 0:1] * (scaled - first - standard * cross)
-        dxs[k] = value.astype(BF16)
-        turn(5 + k)
-
+        inverse = rs[k].reshape(32, 128)[:, 0:1]
+        value = g[k, 1, 0].reshape(32, 1024).astype(F32) + inverse * (
+            scaled - first - standard * cross
+        )
+        dxs[k] = value.astype(BF16).reshape(2, 16, 1024)
+        turn(5 + i)
+    ag_out[...] = ag[...]
+    for m in range(1, 8):
+        j = there_of(m)
+        remote(cc_s, cr_r.at[j], gc_s.at[m], gc_r.at[j], sibling).wait_recv()
+    gain_out[...] = cr_r[...].reshape(8, 128)
+    for copy in pending:
+        copy.wait_send()
+
+
+def finish(dxs, sums, dx_out, up_out, down_out):
+    z, yl = lax.axis_index("dp_0"), lax.axis_index("dp_1")
     spot = iota((128, 128), 1)
     tile = spot // 4
     at = tile // 2
@@ -364,52 +434,48 @@
     source = ((z - offset + NZ) & (NZ - 1)) * 2 + (((tile % 2) + yl) & 1)
     perm = (iota((128, 128), 0) == source * 4 + spot % 4).astype(BF16)
     dx_out[...] = nn(perm, dxs[...].reshape(128, 1024)).astype(BF16)
-    up_out[...] = ag[0:16].reshape(256, 1024)
-    down_out[...] = ag[16:32].reshape(256, 1024)
-    for m in range(1, 8):
-        j = there_of(m)
-        remote(cc_s, cr_r.at[j], gc_s.at[m], gc_r.at[j], sibling).wait_recv()
-    gain_out[...] = cr_r[...].reshape(8, 128)
-    for copy in pending:
-        copy.wait_send()
+    up_out[...] = sums[0:32].reshape(256, 1024).astype(F32).T
+    down_out[...] = sums[32:64].reshape(256, 1024).astype(F32)
 
 
 def shards(tokens, cotangent, routes, norm_gain_vector, up_weight, up_bias, down_weight):
     vmem, sem = pltpu.VMEM, pltpu.SemaphoreType.DMA
-    dx, up, down, bias, gain = pl.pallas_call(
+    dxs, sums, bias, gain = pl.pallas_call(
         kernel,
         out_shape=(
-            jax.ShapeDtypeStruct((128, 1024), BF16),
-            jax.ShapeDtypeStruct((256, 1024), BF16),
-            jax.ShapeDtypeStruct((256, 1024), BF16),
+            jax.ShapeDtypeStruct((CHUNKS, 16, 1024), BF16),
+            jax.ShapeDtypeStruct((64, 8, 1024), BF16),
             jax.ShapeDtypeStruct((1, 256), F32),
             jax.ShapeDtypeStruct((8, 128), F32),
         ),
         in_specs=[pl.BlockSpec(memory_space=pltpu.VMEM)] * 7,
-        out_specs=[pl.BlockSpec(memory_space=pltpu.VMEM)] * 5,
+        out_specs=[pl.BlockSpec(memory_space=pltpu.VMEM)] * 4,
         scratch_shapes=[
             vmem((32, 8, 1024), BF16),
             vmem((32, 8, 1024), BF16),
-            vmem((CHUNKS, 2, 8, 32, 1024), BF16),
+            vmem((CHUNKS, 2, 8, 16, 1024), BF16),
             vmem((512, 1024), BF16),
             vmem((512, 1024), BF16),
             vmem((2, 1, 256), F32),
-            vmem((2, 32, 16, 1024), F32),
+            vmem((2, 64, 8, 1024), F32),
             vmem((1, 512), F32),
-            vmem((CHUNKS, 8, 32, 1024), BF16),
-            vmem((8, CHUNKS, 32, 1024), BF16),
-            vmem((CHUNKS, 32, 1024), F32),
-            vmem((CHUNKS, 32, 128), F32),
-            vmem((CHUNKS, 32, 1024), BF16),
-            vmem((16, 2, 16, 1024), BF16),
-            vmem((16, 2, 16, 1024), BF16),
-            vmem((8, 2, 16, 1024), BF16),
-            vmem((8, 2, 16, 1024), BF16),
-            vmem((8, 2, 16, 1024), BF16),
-            vmem((8, 2, 16, 1024), BF16),
-            vmem((2, 16, 1024), BF16),
-            vmem((2, 16, 1024), BF16),
-            vmem((32, 16, 1024), BF16),
+            vmem((CHUNKS, 8, 16, 1024), BF16),
+            vmem((2, 4, 2, 16, 1024), BF16),
+            vmem((2, 4, 2, 16, 1024), BF16),
+            vmem((2, CHUNKS, 2, 16, 1024), BF16),
+            vmem((CHUNKS, 16, 1024), BF16),
+            vmem((CHUNKS, 16, 1024), BF16),
+            vmem((CHUNKS, 16, 1024), F32),
+            vmem((CHUNKS, 16, 128), F32),
+            vmem((16, SUBS, 8, 1024), BF16),
+            vmem((16, SUBS, 8, 1024), BF16),
+            vmem((8, SUBS, 8, 1024), BF16),
+            vmem((8, SUBS, 8, 1024), BF16),
+            vmem((8, SUBS, 8, 1024), BF16),
+            vmem((8, SUBS, 8, 1024), BF16),
+            vmem((SUBS, 8, 1024), BF16),
+            vmem((SUBS, 8, 1024), BF16),
+            vmem((64, 8, 1024), BF16),
             vmem((1, 1280), F32),
             vmem((1, 1280), F32),
             vmem((8, 1, 128), F32),
@@ -422,10 +488,10 @@
             sem((CHUNKS, 7)), sem((CHUNKS, 7)),
             sem((3,)), sem((3,)),
             sem((8,)), sem((8,)),
-            sem((16, 2)), sem((16, 2)),
-            sem((8, 2)), sem((8, 2)), sem((8, 2)), sem((8, 2)),
-            sem((2,)), sem((2,)),
-            sem((8, 2)), sem((8, 2)), sem((8, 2)), sem((8, 2)),
+            sem((16,)), sem((16,)),
+            sem((8, SUBS)), sem((8, SUBS)), sem((8, SUBS)), sem((8, SUBS)),
+            sem((SUBS,)), sem((SUBS,)),
+            sem((8, SUBS)), sem((8, SUBS)), sem((8, SUBS)), sem((8, SUBS)),
             sem((1,)), sem((1,)),
             sem((8,)), sem((8,)),
             sem((32,)), sem((32,)),
@@ -440,17 +506,22 @@
         cotangent,
         routes.reshape(1, -1),
         norm_gain_vector.reshape(1, -1),
-        up_weight.T,
+        up_weight,
         up_bias.reshape(1, -1),
         down_weight,
     )
-    return (
-        dx,
-        up.T.astype(F32),
-        bias.reshape(-1),
-        down.astype(F32),
-        gain.reshape(-1),
-    )
+    dx, up, down = pl.pallas_call(
+        finish,
+        out_shape=(
+            jax.ShapeDtypeStruct((128, 1024), BF16),
+            jax.ShapeDtypeStruct((1024, 256), F32),
+            jax.ShapeDtypeStruct((256, 1024), F32),
+        ),
+        in_specs=[pl.BlockSpec(memory_space=pltpu.VMEM)] * 2,
+        out_specs=[pl.BlockSpec(memory_space=pltpu.VMEM)] * 3,
+        name="finish",
+    )(dxs, sums)
+    return (dx, up, bias.reshape(-1), down, gain.reshape(-1))
 
 
 def solution(mesh):

time: 147 us -> 140 us (0.952)
  the two profiles are of different devices: /device:TPU:18 before, /device:TPU:16 now
where the time goes in v2:
time: 140 us; the launch traced here: 139 us
  Pallas kernels  137 us (98%)
  local copies, waits for them, and re-layouts  1.83 us (1%)
    pallas_call x1, Pallas kernels, shards(): pl.pallas_call(kernel, out_shape=(jax.ShapeDtypeStruct((CHUNKS, 16, 1024)...  134 us
    pallas_call x1, Pallas kernels, shards(): pl.pallas_call(finish, out_shape=(jax.ShapeDtypeStruct((128, 1024), BF16)...  2.99 us

profile of v2, /device:TPU:16, one launch (start us, length us, event | category | flops | bytes accessed | tf_op | source)
XLA Modules:
  0.0 139.5 jit_solution(8746062869593461259)
XLA Ops:
  0.6 134.0 %ffn_backward.1 = (bf16[8,16,1024]{2,1,0:T(8,128)(2,1)}, bf16[64,8,1024]{2,1,0:T(8,128)(2,1)}, f32[1,256]{1,0:T(1,128)}, f32[8,128]{1,0:T(8,128)}) custom-call(bf16[128,1024]{1,0:T(8,128)(2,1)} %tok.1, bf16[128,1024]{1,0:T(8,128)(2,1)} %cot.1, s32[1,128]{1,0:T(1,128)} %bitcast.9, f32[1,1024]{1,0:T(1,128)} %bitcast.5, bf16[1024,256]{1,0:T(8,128)(2,1)} %wu_in.1, ...), custom_call_target="tpu_custom_call" | custom-call | tf_op jit(solution)/shard_map/ffn_backward/pallas_call | solution.py:443
  134.6 3.0 %finish.1 = (bf16[128,1024]{1,0:T(8,128)(2,1)}, f32[1024,256]{1,0:T(8,128)}, f32[256,1024]{1,0:T(8,128)}) custom-call(bf16[8,16,1024]{2,1,0:T(8,128)(2,1)} %get-tuple-element.12.dxs, bf16[64,8,1024]{2,1,0:T(8,128)(2,1)} %get-tuple-element.13.sums), custom_call_target="tpu_custom_call" | custom-call | tf_op jit(solution)/shard_map/finish/pallas_call | solution.py:513
  137.6 0.0 copy-start
  137.6 0.0 copy-start.1
  137.6 0.7 copy-done.1
  138.3 0.6 copy.14
  138.9 0.0 copy-done
  138.9 0.6 copy.15
Async XLA Ops:
  137.6 1.2 copy-start
  137.6 0.7 copy-start.1

commit v3 on v2

--- a/solution.py
+++ b/solution.py
@@ -49,10 +49,10 @@
     tok, cot, routes, gain, wu_in, bu_in, wd_in,
     dxs, ag_out, bias_out, gain_out,
     send, land, g, wu, wd, bu, acc, bacc, part, fars, near_s, near_r, ysend, yrecv, xh, rs,
-    cs, cr, sp, rp, sm, rm, ys, yr, ag,
+    cs, cr, fs, fr, sp, rp, ys, yr, ag,
     small_s, small_r, gs, ar, bs, br, cc_s, cr_r,
     a2a_s, a2a_r, gat_s, gat_r, w_s, w_r, p_s, p_r, cs_s, cs_r,
-    rp_s, rp_r, rm_s, rm_r, y_s, y_r, ap_s, ap_r, am_s, am_r,
+    fd_s, fd_r, rp_s, rp_r, y_s, y_r, ap_s, ap_r, am_s, am_r,
     sm_s, sm_r, ga_s, ga_r, gb_s, gb_r, gc_s, gc_r,
 ):
     z, yl = lax.axis_index("dp_0"), lax.axis_index("dp_1")
@@ -109,25 +109,28 @@
         a2a[t] = go(
             remote(send.at[t], land.at[t], a2a_s.at[t], a2a_r.at[t], zpeer(OFFSETS[t // 2], t % 2))
         )
-    wu[0:256] = wu_in[...].T
     weights = [
-        go(remote(wu.at[0:256], wu.at[256:512], w_s.at[0], w_r.at[0], sibling)),
-        go(remote(wd_in, wd.at[256:512], w_s.at[1], w_r.at[1], sibling)),
-        go(remote(bu_in, bu.at[1], w_s.at[2], w_r.at[2], sibling)),
+        (remote(wu.at[0:256], wu.at[256:512], w_s.at[0], w_r.at[0], sibling)),
+        (remote(wd_in, wd.at[256:512], w_s.at[1], w_r.at[1], sibling)),
+        (remote(bu_in, bu.at[1], w_s.at[2], w_r.at[2], sibling)),
     ]
 
-    moves = [
-        (0, 1, (0, 1)),
-        (0, 6, (1, 0)), (0, 2, (3, 0)),
-        (1, 7, (1, 0)), (1, 3, (3, 0)),
-        (6, 4, (1, 0)), (3, 5, (3, 0)),
-    ]
-
-    def move(k, i):
-        src, dst, (rx, ry) = moves[i]
-        return remote(
-            g.at[k, :, src], g.at[k, :, dst], gat_s.at[k, i], gat_r.at[k, i], xpeer(rx, ry)
-        )
+    STAGED_Y, STAGED_X, DIRECT = 0, 1, 2
+    plan = [STAGED_Y, STAGED_X, STAGED_Y, STAGED_X, STAGED_Y, STAGED_X, STAGED_X, DIRECT]
+    here_now = set()
+
+    def push(k, src, dst, rx, ry):
+        go(
+            remote(
+                g.at[k, :, src], g.at[k, :, dst], gat_s.at[k, dst], gat_r.at[k, dst], xpeer(rx, ry)
+            )
+        )
+
+    def need(k, slot):
+        if (k, slot) not in here_now:
+            here_now.add((k, slot))
+            spot = g.at[k, :, slot]
+            remote(spot, spot, gat_s.at[k, slot], gat_r.at[k, slot], sibling).wait_recv()
 
     sorter = iota((32, 32), 0)
     column = iota((32, 32), 1)
@@ -148,24 +151,39 @@
         rs[k] = jnp.broadcast_to(inverse, (16, 128))
         g[k, 0, 0] = (standard * gain[...]).astype(BF16)
         g[k, 1, 0] = rows[16:32].astype(BF16)
-        for i in range(3):
-            go(move(k, i))
+        if plan[k] == STAGED_Y:
+            push(k, 0, 1, 0, 1)
+            push(k, 0, 6, 1, 0)
+            push(k, 0, 2, 3, 0)
+        elif plan[k] == STAGED_X:
+            push(k, 0, 4, 2, 0)
+            push(k, 0, 6, 1, 0)
+            push(k, 0, 2, 3, 0)
+            push(k, 0, 1, 0, 1)
+        else:
+            for rx, ry in ((2, 1), (1, 1), (3, 1), (0, 1), (2, 0), (1, 0), (3, 0)):
+                push(k, 0, ((NX - rx) % NX) * 2 + ry, rx, ry)
 
     def second(k):
-        move(k, 0).wait_recv()
-        go(move(k, 3))
-        go(move(k, 4))
+        if plan[k] == STAGED_Y:
+            need(k, 1)
+            push(k, 1, 7, 1, 0)
+            push(k, 1, 3, 3, 0)
+        else:
+            for slot in (6, 2, 4):
+                need(k, slot)
+                push(k, slot, slot + 1, 0, 1)
 
     def third(k):
-        move(k, 1).wait_recv()
-        go(move(k, 5))
-        move(k, 4).wait_recv()
-        go(move(k, 6))
+        need(k, 6)
+        push(k, 6, 4, 1, 0)
+        need(k, 3)
+        push(k, 3, 5, 3, 0)
 
     def compute(j, n):
         for k in range(j, j + n):
-            for i in (2, 3, 5, 6):
-                move(k, i).wait_recv()
+            for slot in range(1, 8):
+                need(k, slot)
         normed = g[j : j + n, 0].reshape(128 * n, 1024)
         outer = g[j : j + n, 1].reshape(128 * n, 1024)
         bias = jnp.concatenate([bu[0], bu[1]], axis=1)
@@ -190,10 +208,12 @@
     own(2)
     second(0)
     own(3)
+    wu[0:256] = wu_in[...].T
+    for w in weights:
+        go(w)
     second(1)
+    second(2)
     third(0)
-    second(2)
-    third(1)
     own(4)
     second(3)
     third(2)
@@ -201,25 +221,21 @@
         w.wait_recv()
     compute(0, 2)
     own(5)
-    third(3)
     second(4)
+    compute(2, 2)
     third(4)
-    compute(2, 2)
     own(6)
     second(5)
-    third(5)
+    own(7)
     second(6)
-    own(7)
     compute(4, 2)
-    third(6)
-    second(7)
-    third(7)
-    compute(6, 2)
+    compute(6, 1)
+    compute(7, 1)
 
     def across(r):
         return remote(cs.at[r], cr.at[r], cs_s.at[r], cs_r.at[r], sibling)
 
-    for r in (8, 9, 7, 10, 6, 11, 5, 12, 4, 13, 3, 14, 2, 15, 1, 0):
+    for r in (8, 7, 9, 5, 11, 6, 10, 3, 13, 4, 12, 1, 15, 2, 14, 0):
         o = lax.rem(z + r, NZ)
         cs[r] = acc[1, pl.ds(o * SUBS, SUBS)].astype(BF16)
         go(across(r))
@@ -272,32 +288,55 @@
     def mine(r, h):
         return acc[0, SUBS * lax.rem(z + r, NZ) + h] + cr[r, h].astype(F32)
 
-    def plus(s, h):
-        return remote(sp.at[s, h], rp.at[s, h], rp_s.at[s, h], rp_r.at[s, h], zpeer(1, 0))
-
-    def minus(s, h):
-        return remote(sm.at[s, h], rm.at[s, h], rm_s.at[s, h], rm_r.at[s, h], zpeer(NZ - 1, 0))
-
-    def ring(s):
-        across(8 - s).wait_recv()
-        if s < 7:
-            across(9 + s).wait_recv()
+    ways = (0, 1)
+
+    def toward(way, d):
+        return d if way == 0 else NZ - d
+
+    def feed(way, d):
+        return remote(
+            fs.at[way, d // 2], fr.at[way, d // 2], fd_s.at[way, d // 2], fd_r.at[way, d // 2],
+            zpeer(toward(way, 1), 0),
+        )
+
+    def chain(way, d, h):
+        i = d // 2 - 1
+        return remote(
+            sp.at[way, i, h], rp.at[way, i, h], rp_s.at[way, i, h], rp_r.at[way, i, h],
+            zpeer(toward(way, 2), 0),
+        )
+
+    def feeders(d):
+        for way in ways:
+            r = toward(way, d)
+            across(r).wait_recv()
+            for h in range(SUBS):
+                fs[way, d // 2, h] = mine(r, h).astype(BF16)
+            go(feed(way, d))
+
+    def links(d):
+        for way in ways:
+            if d == 8 and way:
+                continue
+            across(toward(way, d)).wait_recv()
+            if d < 8:
+                feed(way, d + 1).wait_recv()
         for h in range(SUBS):
-            value = mine(8 - s, h)
-            if s:
-                plus(s - 1, h).wait_recv()
-                value = value + rp[s - 1, h].astype(F32)
-            sp[s, h] = value.astype(BF16)
-            go(plus(s, h))
-            if s < 7:
-                value = mine(9 + s, h)
-                if s:
-                    minus(s - 1, h).wait_recv()
-                    value = value + rm[s - 1, h].astype(F32)
-                sm[s, h] = value.astype(BF16)
-                go(minus(s, h))
-
-    ring(0)
+            for way in ways:
+                if d == 8 and way:
+                    continue
+                value = mine(toward(way, d), h)
+                if d < 8:
+                    value = value + fr[way, d // 2, h].astype(F32)
+                if d < (8 if way == 0 else 6):
+                    chain(way, d + 2, h).wait_recv()
+                    value = value + rp[way, d // 2, h].astype(F32)
+                sp[way, d // 2 - 1, h] = value.astype(BF16)
+                go(chain(way, d, h))
+
+    links(8)
+    feeders(7)
+    feeders(5)
     weighted = jnp.zeros((1, 1024), F32)
     for half in range(2):
         prod = acc[half, 0:32].reshape(256, 1024) * wu[256 * half : 256 * half + 256].astype(F32)
@@ -306,7 +345,8 @@
     small_s[:, 0:1024] = weighted
     small_s[:, 1024:1280] = bacc[:, 256:512]
     to_sibling = go(remote(small_s, small_r, sm_s.at[0], sm_r.at[0], sibling))
-    ring(1)
+    links(6)
+    feeders(3)
     to_sibling.wait_recv()
     whole_gain = weighted + small_r[:, 0:1024]
     for j in range(8):
@@ -324,10 +364,9 @@
                 gs.at[there_of(m)], ar.at[here], ga_s.at[m], ga_r.at[here], xpeer(m // 2, m % 2)
             )
         )
-    ring(2)
-    ring(3)
+    links(4)
+    feeders(1)
     along_plus()
-    ring(4)
     along_minus()
     for m in range(1, 8):
         j = there_of(m)
@@ -341,50 +380,56 @@
                 bs, br.at[number], gb_s.at[t], gb_r.at[number], zpeer(OFFSETS[t // 2], t % 2)
             )
         )
-    for s in range(5, 8):
-        ring(s)
+    links(2)
 
     def swap(h):
         return remote(ys.at[h], yr.at[h], y_s.at[h], y_r.at[h], zpeer(0, 1))
 
     across(0).wait_recv()
+    for way in ways:
+        feed(way, 1).wait_recv()
     for h in range(SUBS):
-        plus(7, h).wait_recv()
-        minus(6, h).wait_recv()
-        total = mine(0, h) + rp[7, h].astype(F32) + rm[6, h].astype(F32)
+        total = mine(0, h)
+        for way in ways:
+            chain(way, 2, h).wait_recv()
+            total = total + rp[way, 0, h].astype(F32) + fr[way, 0, h].astype(F32)
         ys[h] = total.astype(BF16)
         go(swap(h))
-    across_y()
-
-    def spread(s, h, sign):
-        origin = lax.rem(z + NZ - sign * s, NZ)
-        spot = ag.at[SUBS * origin + h]
-        if sign > 0:
-            return remote(spot, spot, ap_s.at[s, h], ap_r.at[s, h], zpeer(1, 0))
-        return remote(spot, spot, am_s.at[s, h], am_r.at[s, h], zpeer(NZ - 1, 0))
-
-    def arrived(s, h, sign):
-        origin = lax.rem(z + NZ - sign * (s + 1), NZ)
-        spot = ag.at[SUBS * origin + h]
-        if sign > 0:
-            return remote(spot, spot, ap_s.at[s, h], ap_r.at[s, h], zpeer(1, 0))
-        return remote(spot, spot, am_s.at[s, h], am_r.at[s, h], zpeer(NZ - 1, 0))
+
+    def spots(way, d, h, n):
+        origin = lax.rem(z + toward(1 - way, d), NZ)
+        return ag.at[pl.ds(SUBS * origin + h, n)]
+
+    def stride(way, d, h, at):
+        spot = spots(way, at, h, 1)
+        i = d // 2 - 1
+        return remote(
+            spot, spot, ap_s.at[way, i, h], ap_r.at[way, i, h], zpeer(toward(way, 2), 0)
+        )
+
+    def single(way, d, at):
+        spot = spots(way, at, 0, SUBS)
+        i = d // 2
+        return remote(spot, spot, am_s.at[way, i], am_r.at[way, i], zpeer(toward(way, 1), 0))
 
     for h in range(SUBS):
         swap(h).wait_recv()
         ag[SUBS * z + h] = (ys[h].astype(F32) + yr[h].astype(F32)).astype(BF16)
-        go(spread(0, h, 1))
-        go(spread(0, h, -1))
-
-    def turn(s):
+        for way in ways:
+            go(stride(way, 2, h, 0))
+    for way in ways:
+        go(single(way, 1, 0))
+    across_y()
+
+    def turn(d):
         for h in range(SUBS):
-            for sign in (1, -1):
-                if sign > 0 or s < 8:
-                    arrived(s - 1, h, sign).wait_recv()
-                    if s < (8 if sign > 0 else 7):
-                        go(spread(s, h, sign))
-
-    turn(1)
+            for way in ways:
+                stride(way, d, h, d).wait_recv()
+                if d < (8 if way == 0 else 6):
+                    go(stride(way, d + 2, h, d))
+        for way in ways:
+            go(single(way, d + 1, d))
+
     for t in range(1, 32):
         source = lax.rem(z + OFFSETS[t // 2], NZ) * 2 + (yl + t % 2) % 2
         remote(bs, br.at[source], gb_s.at[t], gb_r.at[source], sibling).wait_recv()
@@ -394,8 +439,9 @@
     cr_r[here] = sums[:, 0:128]
     for m in range(1, 8):
         go(remote(cc_s, cr_r.at[here], gc_s.at[m], gc_r.at[here], xpeer(m // 2, m % 2)))
-    for s in range(2, 5):
-        turn(s)
+    turn(2)
+    turn(4)
+    turn(6)
 
     last_leg().wait_recv()
     for i in range(4):
@@ -415,7 +461,11 @@
             scaled - first - standard * cross
         )
         dxs[k] = value.astype(BF16).reshape(2, 16, 1024)
-        turn(5 + i)
+    for way in ways:
+        for d in (1, 3, 5, 7):
+            single(way, d, d).wait_recv()
+    for h in range(SUBS):
+        stride(0, 8, h, 8).wait_recv()
     ag_out[...] = ag[...]
     for m in range(1, 8):
         j = there_of(m)
@@ -469,10 +519,10 @@
             vmem((CHUNKS, 16, 128), F32),
             vmem((16, SUBS, 8, 1024), BF16),
             vmem((16, SUBS, 8, 1024), BF16),
-            vmem((8, SUBS, 8, 1024), BF16),
-            vmem((8, SUBS, 8, 1024), BF16),
-            vmem((8, SUBS, 8, 1024), BF16),
-            vmem((8, SUBS, 8, 1024), BF16),
+            vmem((2, 4, SUBS, 8, 1024), BF16),
+            vmem((2, 4, SUBS, 8, 1024), BF16),
+            vmem((2, 4, SUBS, 8, 1024), BF16),
+            vmem((2, 4, SUBS, 8, 1024), BF16),
             vmem((SUBS, 8, 1024), BF16),
             vmem((SUBS, 8, 1024), BF16),
             vmem((64, 8, 1024), BF16),
@@ -485,13 +535,15 @@
             vmem((1, 128), F32),
             vmem((8, 1, 128), F32),
             sem((32,)), sem((32,)),
-            sem((CHUNKS, 7)), sem((CHUNKS, 7)),
+            sem((CHUNKS, 8)), sem((CHUNKS, 8)),
             sem((3,)), sem((3,)),
             sem((8,)), sem((8,)),
             sem((16,)), sem((16,)),
-            sem((8, SUBS)), sem((8, SUBS)), sem((8, SUBS)), sem((8, SUBS)),
+            sem((2, 4)), sem((2, 4)),
+            sem((2, 4, SUBS)), sem((2, 4, SUBS)),
             sem((SUBS,)), sem((SUBS,)),
-            sem((8, SUBS)), sem((8, SUBS)), sem((8, SUBS)), sem((8, SUBS)),
+            sem((2, 4, SUBS)), sem((2, 4, SUBS)),
+            sem((2, 4)), sem((2, 4)),
             sem((1,)), sem((1,)),
             sem((8,)), sem((8,)),
             sem((32,)), sem((32,)),

time: 140 us -> 121 us (0.86)
  the two profiles are of different devices: /device:TPU:16 before, /device:TPU:8 now
where the time goes in v3:
time: 121 us; the launch traced here: 120 us
  Pallas kernels  118 us (98%)
  local copies, waits for them, and re-layouts  1.83 us (2%)
    pallas_call x1, Pallas kernels, shards(): pl.pallas_call(kernel, out_shape=(jax.ShapeDtypeStruct((CHUNKS, 16, 1024)...  115 us
    pallas_call x1, Pallas kernels, shards(): pl.pallas_call(finish, out_shape=(jax.ShapeDtypeStruct((128, 1024), BF16)...  2.99 us

profile of v3, /device:TPU:8, one launch (start us, length us, event | category | flops | bytes accessed | tf_op | source)
XLA Modules:
  0.0 120.4 jit_solution(16377535175402398776)
XLA Ops:
  0.6 114.9 %ffn_backward.1 = (bf16[8,16,1024]{2,1,0:T(8,128)(2,1)}, bf16[64,8,1024]{2,1,0:T(8,128)(2,1)}, f32[1,256]{1,0:T(1,128)}, f32[8,128]{1,0:T(8,128)}) custom-call(bf16[128,1024]{1,0:T(8,128)(2,1)} %tok.1, bf16[128,1024]{1,0:T(8,128)(2,1)} %cot.1, s32[1,128]{1,0:T(1,128)} %bitcast.9, f32[1,1024]{1,0:T(1,128)} %bitcast.5, bf16[1024,256]{1,0:T(8,128)(2,1)} %wu_in.1, ...), custom_call_target="tpu_custom_call" | custom-call | tf_op jit(solution)/shard_map/ffn_backward/pallas_call | solution.py:493
  115.5 3.0 %finish.1 = (bf16[128,1024]{1,0:T(8,128)(2,1)}, f32[1024,256]{1,0:T(8,128)}, f32[256,1024]{1,0:T(8,128)}) custom-call(bf16[8,16,1024]{2,1,0:T(8,128)(2,1)} %get-tuple-element.12.dxs, bf16[64,8,1024]{2,1,0:T(8,128)(2,1)} %get-tuple-element.13.sums), custom_call_target="tpu_custom_call" | custom-call | tf_op jit(solution)/shard_map/finish/pallas_call | solution.py:565
  118.5 0.0 copy-start
  118.5 0.0 copy-start.1
  118.5 0.7 copy-done.1
  119.2 0.6 copy.14
  119.8 0.0 copy-done
  119.8 0.6 copy.15
Async XLA Ops:
  118.5 1.2 %copy-start = (f32[8,128]{1,0:T(8,128)S(1)}, f32[8,128]{1,0:T(8,128)}, u32[]{:S(2)}) copy-start(f32[8,128]{1,0:T(8,128)} %get-tuple-element.18) | copy-start | bytes 12292
  118.5 0.7 copy-start.1

commit v4 on v3

--- a/solution.py
+++ b/solution.py
@@ -116,7 +116,7 @@
     ]
 
     STAGED_Y, STAGED_X, DIRECT = 0, 1, 2
-    plan = [STAGED_Y, STAGED_X, STAGED_Y, STAGED_X, STAGED_Y, STAGED_X, STAGED_X, DIRECT]
+    plan = [STAGED_Y, STAGED_X, STAGED_Y, STAGED_Y, STAGED_X, STAGED_Y, STAGED_Y, DIRECT]
     here_now = set()
 
     def push(k, src, dst, rx, ry):
@@ -222,12 +222,14 @@
     compute(0, 2)
     own(5)
     second(4)
-    compute(2, 2)
-    third(4)
+    third(3)
     own(6)
     second(5)
+    compute(2, 2)
+    second(6)
     own(7)
-    second(6)
+    third(5)
+    third(6)
     compute(4, 2)
     compute(6, 1)
     compute(7, 1)
@@ -475,17 +477,20 @@
         copy.wait_send()
 
 
-def finish(dxs, sums, dx_out, up_out, down_out):
+def finish(dxs, up, down, bias, gain, dx_out, up_out, down_out, bias_out, gain_out):
     z, yl = lax.axis_index("dp_0"), lax.axis_index("dp_1")
-    spot = iota((128, 128), 1)
+    spot = iota((64, 128), 1)
     tile = spot // 4
     at = tile // 2
     offset = jnp.where(at == 0, 0, jnp.where(at % 2 == 1, (at + 1) // 2, NZ - at // 2))
     source = ((z - offset + NZ) & (NZ - 1)) * 2 + (((tile % 2) + yl) & 1)
-    perm = (iota((128, 128), 0) == source * 4 + spot % 4).astype(BF16)
+    row = iota((64, 128), 0) + 64 * pl.program_id(0)
+    perm = (row == source * 4 + spot % 4).astype(BF16)
     dx_out[...] = nn(perm, dxs[...].reshape(128, 1024)).astype(BF16)
-    up_out[...] = sums[0:32].reshape(256, 1024).astype(F32).T
-    down_out[...] = sums[32:64].reshape(256, 1024).astype(F32)
+    up_out[...] = up[...].reshape(128, 1024).astype(F32).T
+    down_out[...] = down[...].reshape(128, 1024).astype(F32)
+    bias_out[...] = bias[...]
+    gain_out[...] = gain[...]
 
 
 def shards(tokens, cotangent, routes, norm_gain_vector, up_weight, up_bias, down_weight):
@@ -562,17 +567,32 @@
         up_bias.reshape(1, -1),
         down_weight,
     )
-    dx, up, down = pl.pallas_call(
+    dx, up, down, bias, gain = pl.pallas_call(
         finish,
+        grid=(2,),
         out_shape=(
             jax.ShapeDtypeStruct((128, 1024), BF16),
             jax.ShapeDtypeStruct((1024, 256), F32),
             jax.ShapeDtypeStruct((256, 1024), F32),
+            jax.ShapeDtypeStruct((1, 256), F32),
+            jax.ShapeDtypeStruct((8, 128), F32),
         ),
-        in_specs=[pl.BlockSpec(memory_space=pltpu.VMEM)] * 2,
-        out_specs=[pl.BlockSpec(memory_space=pltpu.VMEM)] * 3,
+        in_specs=[
+            pl.BlockSpec((CHUNKS, 16, 1024), lambda i: (0, 0, 0)),
+            pl.BlockSpec((16, 8, 1024), lambda i: (i, 0, 0)),
+            pl.BlockSpec((16, 8, 1024), lambda i: (2 + i, 0, 0)),
+            pl.BlockSpec((1, 256), lambda i: (0, 0)),
+            pl.BlockSpec((8, 128), lambda i: (0, 0)),
+        ],
+        out_specs=[
+            pl.BlockSpec((64, 1024), lambda i: (i, 0)),
+            pl.BlockSpec((1024, 128), lambda i: (0, i)),
+            pl.BlockSpec((128, 1024), lambda i: (i, 0)),
+            pl.BlockSpec((1, 256), lambda i: (0, 0)),
+            pl.BlockSpec((8, 128), lambda i: (0, 0)),
+        ],
         name="finish",
-    )(dxs, sums)
+    )(dxs, sums, sums, bias, gain)
     return (dx, up, bias.reshape(-1), down, gain.reshape(-1))
 
 

time: 121 us -> 118 us (0.975)
  local copies, waits for them, and re-layouts: 1.83 us -> 0 us
    unnamed x6 -> x0, local copies, waits for them, and re-layouts: 1.83 us -> none
where the time goes in v4:
time: 118 us
  Pallas kernels  117 us (99%)
    pallas_call x1, Pallas kernels, shards(): pl.pallas_call(kernel, out_shape=(jax.ShapeDtypeStruct((CHUNKS, 16, 1024)...  114 us
    pallas_call x1, Pallas kernels, shards(): pl.pallas_call(finish, grid=(2,), out_shape=(jax.ShapeDtypeStruct((128, 1...  2.75 us

profile of v4, /device:TPU:8, one launch (start us, length us, event | category | flops | bytes accessed | tf_op | source)
XLA Modules:
  0.0 117.6 jit_solution(9197716371795106553)
XLA Ops:
  0.6 114.2 %ffn_backward.1 = (bf16[8,16,1024]{2,1,0:T(8,128)(2,1)}, bf16[64,8,1024]{2,1,0:T(8,128)(2,1)}, f32[1,256]{1,0:T(1,128)}, f32[8,128]{1,0:T(8,128)}) custom-call(bf16[128,1024]{1,0:T(8,128)(2,1)} %tok.1, bf16[128,1024]{1,0:T(8,128)(2,1)} %cot.1, s32[1,128]{1,0:T(1,128)} %bitcast.7, f32[1,1024]{1,0:T(1,128)} %bitcast.5, bf16[1024,256]{1,0:T(8,128)(2,1)} %wu_in.1, ...), custom_call_target="tpu_custom_call" | custom-call | tf_op jit(solution)/shard_map/ffn_backward/pallas_call | solution.py:498
  114.9 2.8 %finish.1 = (bf16[128,1024]{1,0:T(8,128)(2,1)}, f32[1024,256]{1,0:T(8,128)}, f32[256,1024]{1,0:T(8,128)}, f32[1,256]{1,0:T(1,128)}, f32[8,128]{1,0:T(8,128)}) custom-call(bf16[8,16,1024]{2,1,0:T(8,128)(2,1)} %get-tuple-element.14.dxs, bf16[64,8,1024]{2,1,0:T(8,128)(2,1)} %get-tuple-element.15.up.down, bf16[64,8,1024]{2,1,0:T(8,128)(2,1)} %get-tuple-element.15.up.down, ...), custom_call_target="tpu_custom_call" | custom-call | tf_op jit(solution)/shard_map/finish/pallas_call | solution.py:570

commit v5 on v4

--- a/solution.py
+++ b/solution.py
@@ -51,7 +51,7 @@
     send, land, g, wu, wd, bu, acc, bacc, part, fars, near_s, near_r, ysend, yrecv, xh, rs,
     cs, cr, fs, fr, sp, rp, ys, yr, ag,
     small_s, small_r, gs, ar, bs, br, cc_s, cr_r,
-    a2a_s, a2a_r, gat_s, gat_r, w_s, w_r, p_s, p_r, cs_s, cs_r,
+    a2a_s, a2a_r, gat_s, gat_r, hf_s, hf_r, w_s, w_r, p_s, p_r, cs_s, cs_r,
     fd_s, fd_r, rp_s, rp_r, y_s, y_r, ap_s, ap_r, am_s, am_r,
     sm_s, sm_r, ga_s, ga_r, gb_s, gb_r, gc_s, gc_r,
 ):
@@ -99,8 +99,6 @@
     )
     send[...] = placed.astype(BF16).reshape(32, 8, 1024)
     land[0] = send[0]
-    wd[0:256] = wd_in[...]
-    bu[0] = bu_in[...]
 
     pl.semaphore_wait(barrier, len(peers))
 
@@ -126,11 +124,22 @@
             )
         )
 
+    def half(h, src, dst, peer):
+        rows = pl.ds(8 * h, 8)
+        return remote(
+            g.at[CHUNKS - 1, :, src, rows], g.at[CHUNKS - 1, :, dst, rows],
+            hf_s.at[h, dst], hf_r.at[h, dst], peer,
+        )
+
     def need(k, slot):
         if (k, slot) not in here_now:
             here_now.add((k, slot))
-            spot = g.at[k, :, slot]
-            remote(spot, spot, gat_s.at[k, slot], gat_r.at[k, slot], sibling).wait_recv()
+            if plan[k] == DIRECT:
+                for h in range(2):
+                    half(h, slot, slot, sibling).wait_recv()
+            else:
+                spot = g.at[k, :, slot]
+                remote(spot, spot, gat_s.at[k, slot], gat_r.at[k, slot], sibling).wait_recv()
 
     sorter = iota((32, 32), 0)
     column = iota((32, 32), 1)
@@ -160,9 +169,26 @@
             push(k, 0, 6, 1, 0)
             push(k, 0, 2, 3, 0)
             push(k, 0, 1, 0, 1)
-        else:
-            for rx, ry in ((2, 1), (1, 1), (3, 1), (0, 1), (2, 0), (1, 0), (3, 0)):
-                push(k, 0, ((NX - rx) % NX) * 2 + ry, rx, ry)
+
+    def own_half(h):
+        k, at = CHUNKS - 1, 4 * (CHUNKS - 1) + 2 * h
+        for t in (at, at + 1):
+            a2a[t].wait_recv()
+        order = iota((16, 16), 1)
+        goal = (order // 8) * 4 + (order % 4) + jnp.where(order % 8 >= 4, 8, 0)
+        rows = nn((iota((16, 16), 0) == goal).astype(BF16), land[at : at + 2].reshape(16, 1024))
+        values = rows[0:8]
+        centered = values - jnp.mean(values, axis=1, keepdims=True)
+        variance = jnp.mean(centered * centered, axis=1, keepdims=True)
+        inverse = 1.0 / jnp.sqrt(variance + 1e-05)
+        standard = centered * inverse
+        spot = slice(8 * h, 8 * h + 8)
+        xh[k, spot] = standard
+        rs[k, spot] = jnp.broadcast_to(inverse, (8, 128))
+        g[k, 0, 0, spot] = (standard * gain[...]).astype(BF16)
+        g[k, 1, 0, spot] = rows[8:16].astype(BF16)
+        for rx, ry in ((2, 1), (1, 1), (3, 1), (0, 1), (2, 0), (1, 0), (3, 0)):
+            go(half(h, 0, ((NX - rx) % NX) * 2 + ry, xpeer(rx, ry)))
 
     def second(k):
         if plan[k] == STAGED_Y:
@@ -208,6 +234,8 @@
     own(2)
     second(0)
     own(3)
+    wd[0:256] = wd_in[...]
+    bu[0] = bu_in[...]
     wu[0:256] = wu_in[...].T
     for w in weights:
         go(w)
@@ -226,8 +254,9 @@
     own(6)
     second(5)
     compute(2, 2)
+    own_half(0)
     second(6)
-    own(7)
+    own_half(1)
     third(5)
     third(6)
     compute(4, 2)
@@ -541,6 +570,7 @@
             vmem((8, 1, 128), F32),
             sem((32,)), sem((32,)),
             sem((CHUNKS, 8)), sem((CHUNKS, 8)),
+            sem((2, 8)), sem((2, 8)),
             sem((3,)), sem((3,)),
             sem((8,)), sem((8,)),
             sem((16,)), sem((16,)),

time: 118 us -> 116 us (0.983)
  Pallas kernels: 117 us -> 115 us
    pallas_call x1, Pallas kernels: 114 us -> 113 us  [shards(): pl.pallas_call(kernel, out_shape=(jax.ShapeDtypeStruct((CHUNKS, 16, 1024)...]
where the time goes in v5:
time: 116 us
  Pallas kernels  115 us (99%)
    pallas_call x1, Pallas kernels, shards(): pl.pallas_call(kernel, out_shape=(jax.ShapeDtypeStruct((CHUNKS, 16, 1024)...  113 us
    pallas_call x1, Pallas kernels, shards(): pl.pallas_call(finish, grid=(2,), out_shape=(jax.ShapeDtypeStruct((128, 1...  2.76 us

profile of v5, /device:TPU:8, one launch (start us, length us, event | category | flops | bytes accessed | tf_op | source)
XLA Modules:
  0.0 116.1 jit_solution(1132581499658286905)
XLA Ops:
  0.6 112.7 %ffn_backward.1 = (bf16[8,16,1024]{2,1,0:T(8,128)(2,1)}, bf16[64,8,1024]{2,1,0:T(8,128)(2,1)}, f32[1,256]{1,0:T(1,128)}, f32[8,128]{1,0:T(8,128)}) custom-call(bf16[128,1024]{1,0:T(8,128)(2,1)} %tok.1, bf16[128,1024]{1,0:T(8,128)(2,1)} %cot.1, s32[1,128]{1,0:T(1,128)} %bitcast.7, f32[1,1024]{1,0:T(1,128)} %bitcast.5, bf16[1024,256]{1,0:T(8,128)(2,1)} %wu_in.1, ...), custom_call_target="tpu_custom_call" | custom-call | tf_op jit(solution)/shard_map/ffn_backward/pallas_call | solution.py:527
  113.4 2.8 %finish.1 = (bf16[128,1024]{1,0:T(8,128)(2,1)}, f32[1024,256]{1,0:T(8,128)}, f32[256,1024]{1,0:T(8,128)}, f32[1,256]{1,0:T(1,128)}, f32[8,128]{1,0:T(8,128)}) custom-call(bf16[8,16,1024]{2,1,0:T(8,128)(2,1)} %get-tuple-element.14.dxs, bf16[64,8,1024]{2,1,0:T(8,128)(2,1)} %get-tuple-element.15.up.down, bf16[64,8,1024]{2,1,0:T(8,128)(2,1)} %get-tuple-element.15.up.down, ...), custom_call_target="tpu_custom_call" | custom-call | tf_op jit(solution)/shard_map/finish/pallas_call | solution.py:600
